TPU v7x, 128 devices: a whole 4x4x4 slice. The times are simulated.
128 devices in a mesh: section: 2 (over x_lo), seq: 8 (over y, core), tp: 8 (over z, x_hi).
Axes of the slice: x: 4 (x_hi: 2, x_lo: 2; x = x_hi * 2 + x_lo), y: 4, z: 4, core: 2. Of those that a mesh axis runs over, the one named last changes fastest.
Arguments:
- hidden_image: bfloat16 [2, 1024, 1536], P(None, 'seq'), may hold values from -6 to 6
- hidden_text: bfloat16 [2, 256, 1536], P(None, 'seq'), may hold values from -6 to 6
- latent: float32 [2, 1024, 64], P(None, 'seq'), may hold values from -6 to 6
- timestep: int32 [2], replicated, may hold values from 14 to 27
- text_length: int32 [2], replicated, may hold values from 64 to 154, as said below
- text_keep: int32 [2, 256], replicated, may hold values 0 or 1
- patch_order: int32 [4], replicated, may hold values from 0 to 3, each once
- stale_image_kv: bfloat16 [2, 2, 1024, 2, 1536], P('section', None, 'seq', None, 'tp'), may hold values from -160 to 160
- stale_text_kv: bfloat16 [2, 2, 256, 2, 1536], P('section', None, 'seq', None, 'tp'), may hold values from -6 to 6
- mod_image: float32 [2, 2, 6, 1536], P('section'), may hold values from -3 to 3
- mod_text: float32 [2, 2, 6, 1536], P('section'), may hold values from -3 to 3
- mod_final: float32 [2, 2, 1536], replicated, may hold values from -3 to 3
- qkv_image: bfloat16 [2, 1536, 3, 1536], P('section', None, None, 'tp'), may hold values from -0.15625 to 0.15625
- out_image: bfloat16 [2, 1536, 1536], P('section', 'tp'), may hold values from -0.15625 to 0.15625
- up_image: bfloat16 [2, 1536, 6144], P('section', None, 'tp'), may hold values from -0.15625 to 0.15625
- down_image: bfloat16 [2, 6144, 1536], P('section', 'tp'), may hold values from -0.078125 to 0.078125
- qkv_text: bfloat16 [2, 1536, 3, 1536], P('section', None, None, 'tp'), may hold values from -0.15625 to 0.15625
- out_text: bfloat16 [2, 1536, 1536], P('section', 'tp'), may hold values from -0.15625 to 0.15625
- up_text: bfloat16 [2, 1536, 6144], P('section', None, 'tp'), may hold values from -0.15625 to 0.15625
- down_text: bfloat16 [2, 6144, 1536], P('section', 'tp'), may hold values from -0.078125 to 0.078125
- final_weight: bfloat16 [1536, 64], replicated, may hold values from -0.3125 to 0.3125
Outputs:
- latent_out: float32 [2, 2, 1024, 64], P('section', None, 'seq')
- image_kv_next: bfloat16 [2, 2, 1024, 2, 1536], P('section', None, 'seq', None, 'tp')
- text_kv_next: bfloat16 [2, 2, 256, 2, 1536], P('section', None, 'seq', None, 'tp')
- text_hidden: bfloat16 [2, 2, 256, 1536], P('section', None, 'seq')
Inputs may be any that keep to these rules, and one draw needn't show every extreme that they name: `text_length`: some request has exactly 154 text tokens.
All inputs are finite; a program needn't handle non-finite values.
Results may differ from a plain program's by a relative error of at most 0.023.
Values may be sent and summed in bfloat16 or wider, within the bound.
No kernel may reach another device: no remote copies, remote signals or barrier semaphores. Data moves between devices by JAX's collectives and lax.ppermute only.
A program may use at most 128 MiB of HBM per device.

v0:
```python
import jax
import jax.numpy as jnp
from jax import lax
from jax.sharding import PartitionSpec as P

HD = 64
STEPS = 28
EPSILON = 1e-06
NEGATIVE = -1e30
TIME_SHIFT = 3.0


def passed_along(value, axis, steps):
    count = lax.axis_size(axis)
    initial, last = (max(0, -steps), min(count, count - steps))
    return lax.ppermute(value, axis, [(source, source + steps) for source in range(initial, last)])


def row_norm(values, shift_rows, scale_rows):
    mean_value = jnp.mean(values, axis=-1, keepdims=True)
    centred = values - mean_value
    variance = jnp.mean(centred * centred, axis=-1, keepdims=True)
    return centred * lax.rsqrt(variance + EPSILON) * (1.0 + scale_rows) + shift_rows


def expand_rows(vectors, row_count):
    return jnp.broadcast_to(
        vectors[:, None, :], (vectors.shape[0], row_count, vectors.shape[1])
    ).reshape(-1, vectors.shape[1])


def project(rows, shift_rows, scale_rows, weight):
    flattened = rows.reshape(-1, rows.shape[-1]).astype(jnp.float32)
    normed = row_norm(flattened, shift_rows, scale_rows).astype(jnp.bfloat16)
    mixed = jnp.dot(
        normed, weight.reshape(weight.shape[0], -1), preferred_element_type=jnp.float32
    ).astype(jnp.bfloat16)
    return mixed.reshape(rows.shape[0], rows.shape[1], 3, -1)


def split_heads(values):
    return values.reshape(values.shape[0], values.shape[1], -1, HD)


def block_scores(queries, keys_block, key_mask):
    scores = jnp.einsum(
        "rqhe,rkhe->rhqk", queries, keys_block, preferred_element_type=jnp.float32
    ) * HD ** (-0.5)
    return jnp.where(key_mask[:, None, None, :], scores, NEGATIVE)


def block_weights(scores, rowmax, values_block, key_mask):
    exponent = jnp.where(key_mask[:, None, None, :], jnp.exp(scores - rowmax[..., None]), 0.0)
    totals = jnp.sum(exponent, axis=-1)
    summed = jnp.einsum(
        "rhqk,rkhe->rhqe",
        exponent.astype(jnp.bfloat16),
        values_block,
        preferred_element_type=jnp.float32,
    )
    return (totals, summed)


def heads_out(totals, summed):
    result = summed / totals[..., None]
    merged = jnp.transpose(result, (0, 2, 1, 3))
    return merged.reshape(result.shape[0], result.shape[2], -1).astype(jnp.bfloat16)


def sigma_of(index_value):
    progress = 1.0 - index_value / STEPS
    return TIME_SHIFT * progress / (1.0 + (TIME_SHIFT - 1.0) * progress)


def on_device(
    hidden_image,
    hidden_text,
    latent,
    timestep,
    text_length,
    text_keep,
    patch_order,
    stale_image_kv,
    stale_text_kv,
    mod_image,
    mod_text,
    mod_final,
    qkv_image,
    out_image,
    up_image,
    down_image,
    qkv_text,
    out_text,
    up_text,
    down_text,
    final_weight,
):
    requests = hidden_image.shape[0]
    model_width = hidden_image.shape[2]
    slot_count = patch_order.shape[0]
    image_local = hidden_image.shape[1]
    text_local = hidden_text.shape[1]
    patch_rows = image_local // slot_count
    group_rows = text_local // slot_count
    slot_rows = patch_rows + group_rows
    local_width = qkv_image.shape[3]
    seq_count = lax.axis_size("seq")
    section_index = lax.axis_index("section")
    first_section = section_index == 0
    text_total = text_keep.shape[1]
    positions = jnp.arange(text_total, dtype=jnp.int32)
    valid_text = (positions[None, :] < text_length[:, None]) & (text_keep == 1)
    stale_image, stale_text = (
        lax.all_gather(stale_image_kv[0], "seq", axis=1, tiled=True),
        lax.all_gather(stale_text_kv[0], "seq", axis=1, tiled=True),
    )
    image_buffer = stale_image.reshape(requests, seq_count, slot_count, patch_rows, 2, local_width)
    text_buffer = stale_text.reshape(requests, seq_count, slot_count, group_rows, 2, local_width)
    image_mrows = [expand_rows(mod_image[0][:, column], patch_rows) for column in range(6)]
    text_mrows = [expand_rows(mod_text[0][:, column], group_rows) for column in range(6)]
    image_input = hidden_image.reshape(requests, slot_count, patch_rows, model_width)
    text_input = hidden_text.reshape(requests, slot_count, group_rows, model_width)
    image_store = jnp.zeros((requests, slot_count, patch_rows, model_width), jnp.bfloat16)
    text_store = jnp.zeros((requests, slot_count, group_rows, model_width), jnp.bfloat16)
    image_kv_store = jnp.zeros((requests, slot_count, patch_rows, 2, local_width), jnp.bfloat16)
    text_kv_store = jnp.zeros((requests, slot_count, group_rows, 2, local_width), jnp.bfloat16)
    arrived_image = jnp.zeros((requests, patch_rows, model_width), jnp.bfloat16)
    arrived_text = jnp.zeros((requests, group_rows, model_width), jnp.bfloat16)
    for moment in range(slot_count + 1):
        slot_raw = moment - section_index
        in_range = (slot_raw >= 0) & (slot_raw < slot_count)
        slot_index = jnp.clip(slot_raw, 0, slot_count - 1)
        patch_index = lax.dynamic_index_in_dim(patch_order, slot_index, 0, keepdims=False)
        image_rows = jnp.where(
            first_section,
            lax.dynamic_index_in_dim(image_input, patch_index, 1, keepdims=False),
            arrived_image,
        )
        text_rows = jnp.where(
            first_section,
            lax.dynamic_index_in_dim(text_input, slot_index, 1, keepdims=False),
            arrived_text,
        )
        image_qkv = project(image_rows, image_mrows[0], image_mrows[1], qkv_image[0])
        text_qkv = project(text_rows, text_mrows[0], text_mrows[1], qkv_text[0])
        fresh_local = jnp.concatenate([image_qkv[:, :, 1:], text_qkv[:, :, 1:]], axis=1)
        queries = split_heads(jnp.concatenate([image_qkv[:, :, 0], text_qkv[:, :, 0]], axis=1))
        fresh_all = lax.all_gather(fresh_local, "seq", axis=1, tiled=True)
        fresh_split = fresh_all.reshape(requests, seq_count, slot_rows, 2, local_width)
        image_buffer = lax.dynamic_update_slice_in_dim(
            image_buffer, fresh_split[:, :, None, :patch_rows], patch_index, axis=2
        )
        text_buffer = lax.dynamic_update_slice_in_dim(
            text_buffer, fresh_split[:, :, None, patch_rows:], slot_index, axis=2
        )
        image_keys = image_buffer.reshape(requests, -1, 2, local_width)
        text_keys = text_buffer.reshape(requests, -1, 2, local_width)
        image_mask = jnp.ones((requests, image_keys.shape[1]), jnp.bool_)
        image_scores = block_scores(queries, split_heads(image_keys[:, :, 0]), image_mask)
        text_scores = block_scores(queries, split_heads(text_keys[:, :, 0]), valid_text)
        rowmax = jnp.maximum(jnp.max(image_scores, axis=-1), jnp.max(text_scores, axis=-1))
        image_totals, image_summed = block_weights(
            image_scores, rowmax, split_heads(image_keys[:, :, 1]), image_mask
        )
        text_totals, text_summed = block_weights(
            text_scores, rowmax, split_heads(text_keys[:, :, 1]), valid_text
        )
        attended = heads_out(image_totals + text_totals, image_summed + text_summed)
        image_part = jnp.dot(
            attended[:, :patch_rows].reshape(-1, local_width),
            out_image[0],
            preferred_element_type=jnp.float32,
        )
        text_part = jnp.dot(
            attended[:, patch_rows:].reshape(-1, local_width),
            out_text[0],
            preferred_element_type=jnp.float32,
        )
        image_flat = image_rows.reshape(-1, model_width).astype(jnp.float32)
        text_flat = text_rows.reshape(-1, model_width).astype(jnp.float32)
        image_sum, text_sum = (
            lax.psum(image_part.astype(jnp.bfloat16), "tp").astype(jnp.float32),
            lax.psum(text_part.astype(jnp.bfloat16), "tp").astype(jnp.float32),
        )
        image_first = image_flat + image_mrows[2] * image_sum
        text_first = text_flat + text_mrows[2] * text_sum
        image_normed = row_norm(image_first, image_mrows[3], image_mrows[4]).astype(jnp.bfloat16)
        text_normed = row_norm(text_first, text_mrows[3], text_mrows[4]).astype(jnp.bfloat16)
        image_hidden = jax.nn.gelu(
            jnp.dot(image_normed, up_image[0], preferred_element_type=jnp.float32), approximate=True
        ).astype(jnp.bfloat16)
        text_hidden_rows = jax.nn.gelu(
            jnp.dot(text_normed, up_text[0], preferred_element_type=jnp.float32), approximate=True
        ).astype(jnp.bfloat16)
        image_down, text_down = (
            lax.psum(
                jnp.dot(image_hidden, down_image[0], preferred_element_type=jnp.float32).astype(
                    jnp.bfloat16
                ),
                "tp",
            ).astype(jnp.float32),
            lax.psum(
                jnp.dot(text_hidden_rows, down_text[0], preferred_element_type=jnp.float32).astype(
                    jnp.bfloat16
                ),
                "tp",
            ).astype(jnp.float32),
        )
        image_new = (image_first + image_mrows[5] * image_down).astype(jnp.bfloat16)
        text_new = (text_first + text_mrows[5] * text_down).astype(jnp.bfloat16)
        image_new_rows = image_new.reshape(requests, patch_rows, model_width)
        text_new_rows = text_new.reshape(requests, group_rows, model_width)
        image_store = jnp.where(
            in_range,
            lax.dynamic_update_index_in_dim(image_store, image_new_rows, patch_index, 1),
            image_store,
        )
        text_store = jnp.where(
            in_range,
            lax.dynamic_update_index_in_dim(text_store, text_new_rows, slot_index, 1),
            text_store,
        )
        image_kv_store = jnp.where(
            in_range,
            lax.dynamic_update_index_in_dim(image_kv_store, image_qkv[:, :, 1:], patch_index, 1),
            image_kv_store,
        )
        text_kv_store = jnp.where(
            in_range,
            lax.dynamic_update_index_in_dim(text_kv_store, text_qkv[:, :, 1:], slot_index, 1),
            text_kv_store,
        )
        if moment < slot_count:
            arrived_image, arrived_text = passed_along(
                (image_new_rows, text_new_rows), "section", 1
            )
    final_rows = image_store.reshape(-1, model_width).astype(jnp.float32)
    final_normed = row_norm(
        final_rows,
        expand_rows(mod_final[:, 0], image_local),
        expand_rows(mod_final[:, 1], image_local),
    ).astype(jnp.bfloat16)
    velocity = jnp.dot(final_normed, final_weight, preferred_element_type=jnp.float32).reshape(
        requests, image_local, -1
    )
    returned = passed_along(velocity.astype(jnp.bfloat16), "section", -1).astype(velocity.dtype)
    velocity_used = jnp.where(first_section, returned, velocity)
    index_value = timestep.astype(jnp.float32)
    sigma_now = sigma_of(index_value)
    sigma_next = sigma_of(index_value + 1.0)
    stepped = latent + (sigma_next - sigma_now)[:, None, None] * velocity_used
    denoised = latent - sigma_now[:, None, None] * velocity_used
    latent_part = jnp.where(first_section, stepped, denoised)[None]
    return (
        latent_part,
        image_kv_store.reshape(requests, image_local, 2, local_width)[None],
        text_kv_store.reshape(requests, text_local, 2, local_width)[None],
        text_store.reshape(requests, text_local, model_width)[None],
    )


def solution(mesh):
    in_specs = (
        P(None, "seq", None),
        P(None, "seq", None),
        P(None, "seq", None),
        P(),
        P(),
        P(),
        P(),
        P("section", None, "seq", None, "tp"),
        P("section", None, "seq", None, "tp"),
        P("section", None, None, None),
        P("section", None, None, None),
        P(),
        P("section", None, None, "tp"),
        P("section", "tp", None),
        P("section", None, "tp"),
        P("section", "tp", None),
        P("section", None, None, "tp"),
        P("section", "tp", None),
        P("section", None, "tp"),
        P("section", "tp", None),
        P(),
    )
    out_specs = (
        P("section", None, "seq", None),
        P("section", None, "seq", None, "tp"),
        P("section", None, "seq", None, "tp"),
        P("section", None, "seq", None),
    )
    return jax.shard_map(
        on_device, mesh=mesh, in_specs=in_specs, out_specs=out_specs, check_vma=False
    )
```

profile of v0, /device:TPU:2, one launch (start us, length us, event | category | flops | bytes accessed | tf_op | source)
XLA Modules:
  0.0 1606.8 jit_solution(7978806751904991760)
XLA Ops:
  25.3 14.3 all-gather.1
  94.2 42.6 %psum.142 = bf16[16,1536]{1,0:T(8,128)(2,1)S(1)} all-reduce(bf16[16,1536]{1,0:T(8,128)(2,1)S(1)} %convolution_convert_fusion.9), channel_id=1, replica_groups=mesh['section'=2,'seq'=8,'tp'=8] {'tp'}, use_global_device_ids=true, to_apply=%region_14.15 | all-reduce | flops 24576 | bytes 98304 | tf_op jit(solution)/shard_map/psum | solution.py:183
  140.6 38.1 %psum.143 = bf16[16,1536]{1,0:T(8,128)(2,1)} all-reduce(bf16[16,1536]{1,0:T(8,128)(2,1)S(1)} %fusion.55), channel_id=1, replica_groups=mesh['section'=2,'seq'=8,'tp'=8] {'tp'}, use_global_device_ids=true, to_apply=%region_17.18 | all-reduce | flops 24576 | bytes 98304 | tf_op jit(solution)/shard_map/psum | solution.py:202
  191.2 77.5 %all-reduce.11.cloned.1.call-done = bf16[64,1536]{1,0:T(8,128)(2,1)} async-done(((bf16[64,1536]{1,0:T(8,128)(2,1)}), bf16[64,1536]{1,0:T(8,128)(2,1)}) %all-reduce.11.cloned.1.call-update) | async-done | bytes 196624 | tf_op jit(solution)/shard_map/psum | solution.py:182
  276.6 81.9 %all-reduce.13.cloned.1.call-done = bf16[64,1536]{1,0:T(8,128)(2,1)} async-done(((bf16[64,1536]{1,0:T(8,128)(2,1)}), bf16[64,1536]{1,0:T(8,128)(2,1)}) %all-reduce.13.cloned.1.call-update) | async-done | bytes 196624 | tf_op jit(solution)/shard_map/psum | solution.py:196
  372.8 13.6 all_gather.24
  414.5 39.5 %psum.146 = bf16[16,1536]{1,0:T(8,128)(2,1)S(1)} all-reduce(bf16[16,1536]{1,0:T(8,128)(2,1)S(1)} %convolution_convert_fusion.8), channel_id=1, replica_groups=mesh['section'=2,'seq'=8,'tp'=8] {'tp'}, use_global_device_ids=true, to_apply=%region_30.31 | all-reduce | flops 24576 | bytes 98304 | tf_op jit(solution)/shard_map/psum | solution.py:183
  458.4 40.0 %psum.147 = bf16[16,1536]{1,0:T(8,128)(2,1)} all-reduce(bf16[16,1536]{1,0:T(8,128)(2,1)} %fusion.58), channel_id=1, replica_groups=mesh['section'=2,'seq'=8,'tp'=8] {'tp'}, use_global_device_ids=true, to_apply=%region_33.34 | all-reduce | flops 24576 | bytes 98304 | tf_op jit(solution)/shard_map/psum | solution.py:202
  510.7 77.7 %all-reduce.15.cloned.1.call-done = bf16[64,1536]{1,0:T(8,128)(2,1)} async-done(((bf16[64,1536]{1,0:T(8,128)(2,1)}), bf16[64,1536]{1,0:T(8,128)(2,1)}) %all-reduce.15.cloned.1.call-update) | async-done | bytes 196624 | tf_op jit(solution)/shard_map/psum | solution.py:182
  597.5 80.7 %all-reduce.17.cloned.1.call-done = bf16[64,1536]{1,0:T(8,128)(2,1)} async-done(((bf16[64,1536]{1,0:T(8,128)(2,1)}), bf16[64,1536]{1,0:T(8,128)(2,1)}) %all-reduce.17.cloned.1.call-update) | async-done | bytes 196624 | tf_op jit(solution)/shard_map/psum | solution.py:196
  692.5 13.8 all_gather.25
  734.4 39.5 %psum.150 = bf16[16,1536]{1,0:T(8,128)(2,1)S(1)} all-reduce(bf16[16,1536]{1,0:T(8,128)(2,1)S(1)} %convolution_convert_fusion.7), channel_id=1, replica_groups=mesh['section'=2,'seq'=8,'tp'=8] {'tp'}, use_global_device_ids=true, to_apply=%region_46.47 | all-reduce | flops 24576 | bytes 98304 | tf_op jit(solution)/shard_map/psum | solution.py:183
  778.3 40.0 %psum.151 = bf16[16,1536]{1,0:T(8,128)(2,1)} all-reduce(bf16[16,1536]{1,0:T(8,128)(2,1)} %fusion.61), channel_id=1, replica_groups=mesh['section'=2,'seq'=8,'tp'=8] {'tp'}, use_global_device_ids=true, to_apply=%region_49.50 | all-reduce | flops 24576 | bytes 98304 | tf_op jit(solution)/shard_map/psum | solution.py:202
  830.6 77.7 %all-reduce.19.cloned.1.call-done = bf16[64,1536]{1,0:T(8,128)(2,1)} async-done(((bf16[64,1536]{1,0:T(8,128)(2,1)}), bf16[64,1536]{1,0:T(8,128)(2,1)}) %all-reduce.19.cloned.1.call-update) | async-done | bytes 196624 | tf_op jit(solution)/shard_map/psum | solution.py:182
  917.3 80.7 %all-reduce.21.cloned.1.call-done = bf16[64,1536]{1,0:T(8,128)(2,1)} async-done(((bf16[64,1536]{1,0:T(8,128)(2,1)}), bf16[64,1536]{1,0:T(8,128)(2,1)}) %all-reduce.21.cloned.1.call-update) | async-done | bytes 196624 | tf_op jit(solution)/shard_map/psum | solution.py:196
  1054.0 39.7 %psum.154 = bf16[16,1536]{1,0:T(8,128)(2,1)S(1)} all-reduce(bf16[16,1536]{1,0:T(8,128)(2,1)S(1)} %convolution_convert_fusion.6), channel_id=1, replica_groups=mesh['section'=2,'seq'=8,'tp'=8] {'tp'}, use_global_device_ids=true, to_apply=%region_62.63 | all-reduce | flops 24576 | bytes 98304 | tf_op jit(solution)/shard_map/psum | solution.py:183
  1098.2 40.0 %psum.155 = bf16[16,1536]{1,0:T(8,128)(2,1)} all-reduce(bf16[16,1536]{1,0:T(8,128)(2,1)} %fusion.64), channel_id=1, replica_groups=mesh['section'=2,'seq'=8,'tp'=8] {'tp'}, use_global_device_ids=true, to_apply=%region_65.66 | all-reduce | flops 24576 | bytes 98304 | tf_op jit(solution)/shard_map/psum | solution.py:202
  1149.1 79.0 %all-reduce.23.cloned.1.call-done = bf16[64,1536]{1,0:T(8,128)(2,1)} async-done(((bf16[64,1536]{1,0:T(8,128)(2,1)}), bf16[64,1536]{1,0:T(8,128)(2,1)}) %all-reduce.23.cloned.1.call-update) | async-done | bytes 196624 | tf_op jit(solution)/shard_map/psum | solution.py:182
  1238.0 79.9 %all-reduce.25.cloned.1.call-done = bf16[64,1536]{1,0:T(8,128)(2,1)} async-done(((bf16[64,1536]{1,0:T(8,128)(2,1)}), bf16[64,1536]{1,0:T(8,128)(2,1)}) %all-reduce.25.cloned.1.call-update) | async-done | bytes 196624 | tf_op jit(solution)/shard_map/psum | solution.py:196
  1332.2 13.6 all_gather.27
  1374.0 39.5 %psum.158 = bf16[16,1536]{1,0:T(8,128)(2,1)S(1)} all-reduce(bf16[16,1536]{1,0:T(8,128)(2,1)S(1)} %convolution_convert_fusion.5), channel_id=1, replica_groups=mesh['section'=2,'seq'=8,'tp'=8] {'tp'}, use_global_device_ids=true, to_apply=%region_78.79 | all-reduce | flops 24576 | bytes 98304 | tf_op jit(solution)/shard_map/psum | solution.py:183
  1419.9 39.8 %psum.159 = bf16[16,1536]{1,0:T(8,128)(2,1)} all-reduce(bf16[16,1536]{1,0:T(8,128)(2,1)} %fusion.67), channel_id=1, replica_groups=mesh['section'=2,'seq'=8,'tp'=8] {'tp'}, use_global_device_ids=true, to_apply=%region_81.82 | all-reduce | flops 24576 | bytes 98304 | tf_op jit(solution)/shard_map/psum | solution.py:202
  1459.7 36.9 %all-reduce.27.cloned.1.call-done = bf16[64,1536]{1,0:T(8,128)(2,1)} async-done(((bf16[64,1536]{1,0:T(8,128)(2,1)}), bf16[64,1536]{1,0:T(8,128)(2,1)}) %all-reduce.27.cloned.1.call-update) | async-done | bytes 196624 | tf_op jit(solution)/shard_map/psum | solution.py:182
  1505.8 80.6 %all-reduce.29.cloned.1.call-done = bf16[64,1536]{1,0:T(8,128)(2,1)} async-done(((bf16[64,1536]{1,0:T(8,128)(2,1)}), bf16[64,1536]{1,0:T(8,128)(2,1)}) %all-reduce.29.cloned.1.call-update) | async-done | bytes 196624 | tf_op jit(solution)/shard_map/psum | solution.py:196
  (591 shorter events, 374.8 us)
Async XLA Ops:
  7.2 265.6 %copy-start = (bf16[1,768,1536]{2,1,0:T(8,128)(2,1)S(1)}, bf16[1,768,1536]{2,1,0:T(8,128)(2,1)}, u32[]{:S(2)}) copy-start(bf16[1,768,1536]{2,1,0:T(8,128)(2,1)} %param.36) | copy-start | bytes 7077892
  7.2 73.1 %all-gather.4.cloned.1.call-start = ((), (), s32[]{:S(2)}) async-start(), calls=%async_computation.10 | async-start | bytes 2359296 | tf_op jit(solution)/shard_map/all_gather | solution.py:114
  9.2 259.5 %all-reduce.11.cloned.1.call-start = ((), (), s32[]{:S(2)}) async-start(), calls=%async_computation | async-start | bytes 393216 | tf_op jit(solution)/shard_map/psum | solution.py:182
  180.3 6.3 collective-permute-start.1
  183.3 175.3 %all-reduce.13.cloned.1.call-start = ((), (), s32[]{:S(2)}) async-start(), calls=%async_computation.1 | async-start | bytes 393216 | tf_op jit(solution)/shard_map/psum | solution.py:196
  276.5 312.0 %all-reduce.15.cloned.1.call-start = ((), (), s32[]{:S(2)}) async-start(), calls=%async_computation.2 | async-start | bytes 393216 | tf_op jit(solution)/shard_map/psum | solution.py:182
  359.7 7.6 collective-permute-start
  458.4 132.2 %copy-start.74 = (f32[2,1536]{1,0:T(2,128)S(1)}, f32[2,1536]{1,0:T(2,128)}, u32[]{:S(2)}) copy-start(f32[2,1536]{1,0:T(2,128)} %get-tuple-element.117) | copy-start | bytes 36868
  458.4 132.3 %copy-start.79 = (f32[2,1536]{1,0:T(2,128)S(1)}, f32[2,1536]{1,0:T(2,128)}, u32[]{:S(2)}) copy-start(f32[2,1536]{1,0:T(2,128)} %get-tuple-element.118) | copy-start | bytes 36868
  499.9 6.2 collective-permute-start.3
  504.9 173.3 %all-reduce.17.cloned.1.call-start = ((), (), s32[]{:S(2)}) async-start(), calls=%async_computation.3 | async-start | bytes 393216 | tf_op jit(solution)/shard_map/psum | solution.py:196
  596.1 312.2 %all-reduce.19.cloned.1.call-start = ((), (), s32[]{:S(2)}) async-start(), calls=%async_computation.4 | async-start | bytes 393216 | tf_op jit(solution)/shard_map/psum | solution.py:182
  679.4 7.6 collective-permute-start.2
  778.3 132.2 %copy-start.80 = (f32[2,1536]{1,0:T(2,128)S(1)}, f32[2,1536]{1,0:T(2,128)}, u32[]{:S(2)}) copy-start(f32[2,1536]{1,0:T(2,128)} %get-tuple-element.118) | copy-start | bytes 36868
  819.8 6.2 collective-permute-start.5
  824.7 173.2 %all-reduce.21.cloned.1.call-start = ((), (), s32[]{:S(2)}) async-start(), calls=%async_computation.5 | async-start | bytes 393216 | tf_op jit(solution)/shard_map/psum | solution.py:196
  915.9 312.2 %all-reduce.23.cloned.1.call-start = ((), (), s32[]{:S(2)}) async-start(), calls=%async_computation.6 | async-start | bytes 393216 | tf_op jit(solution)/shard_map/psum | solution.py:182
  999.2 7.6 collective-permute-start.4
  1139.6 6.2 collective-permute-start.7
  1144.6 173.3 %all-reduce.25.cloned.1.call-start = ((), (), s32[]{:S(2)}) async-start(), calls=%async_computation.7 | async-start | bytes 393216 | tf_op jit(solution)/shard_map/psum | solution.py:196
  1235.8 260.9 %all-reduce.27.cloned.1.call-start = ((), (), s32[]{:S(2)}) async-start(), calls=%async_computation.8 | async-start | bytes 393216 | tf_op jit(solution)/shard_map/psum | solution.py:182
  1319.1 7.6 collective-permute-start.6
  1415.8 170.6 %all-reduce.29.cloned.1.call-start = ((), (), s32[]{:S(2)}) async-start(), calls=%async_computation.9 | async-start | bytes 393216 | tf_op jit(solution)/shard_map/psum | solution.py:196
  1591.9 7.4 collective-permute-start.8
  (101 other events, 4056.7 us)
Sparse Core Ops, SparseCore 0:
  9.7 28.3 all-gather.3
  183.4 85.3 all-reduce.10
  276.6 81.8 all-reduce.12
  505.0 83.3 all-reduce.14
  596.2 81.8 all-reduce.16
  824.9 83.3 all-reduce.18
  916.0 81.8 all-reduce.20
  1144.7 83.3 all-reduce.22
  1235.9 81.8 all-reduce.24
  1415.9 80.6 all-reduce.26
  1504.5 81.8 all-reduce.28
where the time goes:
time: 1620 us; the launch traced here: 1610 us
  waiting for transfers between devices  784 us (48%)
  blocking collectives  481 us (30%)
  local copies, waits for them, and re-layouts  130 us (8%)
  matrix products  100 us (6%)
  other arithmetic  72.3 us (4%)
  between operations  25.4 us (2%)
    psum x5, waiting for transfers between devices, on_device(): lax.psum(jnp.dot(image_hidden, down_image[0], preferred_element_type=jnp....  404 us
    psum x5, waiting for transfers between devices, on_device(): lax.psum(image_part.astype(jnp.bfloat16), 'tp').astype(jnp.float32)  349 us
    psum x5, blocking collectives, on_device(): lax.psum(text_part.astype(jnp.bfloat16), 'tp').astype(jnp.float32)  201 us
    psum x5, blocking collectives, on_device(): lax.psum(jnp.dot(text_hidden_rows, down_text[0], preferred_element_type=j...  198 us
    all_gather x5, blocking collectives, on_device(): fresh_all = lax.all_gather(fresh_local, 'seq', axis=1, tiled=True)  67.8 us
  transfers between devices with their start and end apart: 20, of which 18 were waited for; matrix products, arithmetic and copies ran while one was open for 5% of the time, Pallas kernels for 0%

commit v1 on v0

--- a/solution.py
+++ b/solution.py
@@ -145,7 +145,24 @@
         text_qkv = project(text_rows, text_mrows[0], text_mrows[1], qkv_text[0])
         fresh_local = jnp.concatenate([image_qkv[:, :, 1:], text_qkv[:, :, 1:]], axis=1)
         queries = split_heads(jnp.concatenate([image_qkv[:, :, 0], text_qkv[:, :, 0]], axis=1))
-        fresh_all = lax.all_gather(fresh_local, "seq", axis=1, tiled=True)
+        ways, here, step = (lax.axis_size("seq"), lax.axis_index("seq"), fresh_local.shape[1])
+        shape = [n * ways if d == 1 else n for d, n in enumerate(fresh_local.shape)]
+        fresh_all = lax.dynamic_update_slice_in_dim(
+            jnp.zeros(shape, fresh_local.dtype), fresh_local, here * step, axis=1
+        )
+        going_up = going_down = fresh_local
+        for far in range(1, ways // 2 + 1):
+            going_up = lax.ppermute(going_up, "seq", [(d, (d + 1) % ways) for d in range(ways)])
+            fresh_all = lax.dynamic_update_slice_in_dim(
+                fresh_all, going_up, (here - far) % ways * step, axis=1
+            )
+            if 2 * far < ways:
+                going_down = lax.ppermute(
+                    going_down, "seq", [(d, (d - 1) % ways) for d in range(ways)]
+                )
+                fresh_all = lax.dynamic_update_slice_in_dim(
+                    fresh_all, going_down, (here + far) % ways * step, axis=1
+                )
         fresh_split = fresh_all.reshape(requests, seq_count, slot_rows, 2, local_width)
         image_buffer = lax.dynamic_update_slice_in_dim(
             image_buffer, fresh_split[:, :, None, :patch_rows], patch_index, axis=2

time: 1620 us -> 1670 us (1.031)
  blocking collectives: 481 us -> 413 us
  local copies, waits for them, and re-layouts: 130 us -> 187 us
  starting transfers between devices: 14.6 us -> 59.2 us
    all_gather x5 -> x0, blocking collectives: 67.8 us -> none  [on_device(): fresh_all = lax.all_gather(fresh_local, 'seq', axis=1, tiled=True)]
    psum x5, waiting for transfers between devices: 404 us -> 359 us  [on_device(): lax.psum(jnp.dot(image_hidden, down_image[0], preferred_element_type=jnp....]
    ppermute x0 -> x35, starting transfers between devices: none -> 44.3 us  [the longest x15 43.9 us: on_device(): lax.ppermute(going_down, 'seq', [(d, (d - 1) % ways) for d in range(ways)])]
    dynamic_update_slice x0 -> x40, local copies, waits for them, and re-layouts: none -> 39.3 us  [the longest x20 17.4 us: on_device(): lax.dynamic_update_slice_in_dim(fresh_all, going_up, (here - far) % ways...]
    psum x5, waiting for transfers between devices: 349 us -> 375 us  [on_device(): lax.psum(image_part.astype(jnp.bfloat16), 'tp').astype(jnp.float32)]
    ppermute x0 -> x35, waiting for transfers between devices: none -> 23.2 us  [the longest x20 22.3 us: on_device(): lax.ppermute(going_up, 'seq', [(d, (d + 1) % ways) for d in range(ways)])]
  transfers between devices with their start and end apart: 20 -> 55, of which waited for: 18 -> 37; matrix products, arithmetic and copies ran while one was open for 5% -> 8% of each run, Pallas kernels for 0% -> 0%
where the time goes in v1:
time: 1670 us; the launch traced here: 1650 us
  waiting for transfers between devices  794 us (48%)
  blocking collectives  413 us (25%)
  local copies, waits for them, and re-layouts  187 us (11%)
  matrix products  102 us (6%)
  other arithmetic  72.7 us (4%)
  starting transfers between devices  59.2 us (4%)
  between operations  25.3 us (2%)
    psum x5, waiting for transfers between devices, on_device(): lax.psum(image_part.astype(jnp.bfloat16), 'tp').astype(jnp.float32)  375 us
    psum x5, waiting for transfers between devices, on_device(): lax.psum(jnp.dot(image_hidden, down_image[0], preferred_element_type=jnp....  359 us
    psum x5, blocking collectives, on_device(): lax.psum(text_part.astype(jnp.bfloat16), 'tp').astype(jnp.float32)  201 us
    psum x5, blocking collectives, on_device(): lax.psum(jnp.dot(text_hidden_rows, down_text[0], preferred_element_type=j...  198 us
    ppermute x15, starting transfers between devices, on_device(): lax.ppermute(going_down, 'seq', [(d, (d - 1) % ways) for d in range(ways)])  43.9 us
    ppermute x9, waiting for transfers between devices, passed_along(): lax.ppermute(value, axis, [(source, source + steps) for source in range(i...  36.8 us
  transfers between devices with their start and end apart: 55, of which 37 were waited for; matrix products, arithmetic and copies ran while one was open for 8% of the time, Pallas kernels for 0%

profile of v1, /device:TPU:2, one launch (start us, length us, event | category | flops | bytes accessed | tf_op | source)
XLA Modules:
  0.0 1653.7 jit_solution(13675003534327708894)
XLA Ops:
  34.2 13.9 all-gather.1
  96.0 42.8 %psum.142 = bf16[16,1536]{1,0:T(8,128)(2,1)S(1)} all-reduce(bf16[16,1536]{1,0:T(8,128)(2,1)S(1)} %convolution_convert_fusion.9), channel_id=1, replica_groups=mesh['section'=2,'seq'=8,'tp'=8] {'tp'}, use_global_device_ids=true, to_apply=%region_14.15 | all-reduce | flops 24576 | bytes 98304 | tf_op jit(solution)/shard_map/psum | solution.py:200
  142.7 38.1 %psum.143 = bf16[16,1536]{1,0:T(8,128)(2,1)} all-reduce(bf16[16,1536]{1,0:T(8,128)(2,1)S(1)} %fusion.55), channel_id=1, replica_groups=mesh['section'=2,'seq'=8,'tp'=8] {'tp'}, use_global_device_ids=true, to_apply=%region_17.18 | all-reduce | flops 24576 | bytes 98304 | tf_op jit(solution)/shard_map/psum | solution.py:219
  193.1 75.8 %all-reduce.11.cloned.1.call-done = bf16[64,1536]{1,0:T(8,128)(2,1)} async-done(((bf16[64,1536]{1,0:T(8,128)(2,1)}), bf16[64,1536]{1,0:T(8,128)(2,1)}) %all-reduce.11.cloned.1.call-update) | async-done | bytes 196624 | tf_op jit(solution)/shard_map/psum | solution.py:199
  279.4 79.2 %all-reduce.13.cloned.1.call-done = bf16[64,1536]{1,0:T(8,128)(2,1)} async-done(((bf16[64,1536]{1,0:T(8,128)(2,1)}), bf16[64,1536]{1,0:T(8,128)(2,1)}) %all-reduce.13.cloned.1.call-update) | async-done | bytes 196624 | tf_op jit(solution)/shard_map/psum | solution.py:213
  429.5 39.5 %psum.146 = bf16[16,1536]{1,0:T(8,128)(2,1)S(1)} all-reduce(bf16[16,1536]{1,0:T(8,128)(2,1)S(1)} %convolution_convert_fusion.8), channel_id=1, replica_groups=mesh['section'=2,'seq'=8,'tp'=8] {'tp'}, use_global_device_ids=true, to_apply=%region_30.31 | all-reduce | flops 24576 | bytes 98304 | tf_op jit(solution)/shard_map/psum | solution.py:200
  473.4 39.9 %psum.147 = bf16[16,1536]{1,0:T(8,128)(2,1)} all-reduce(bf16[16,1536]{1,0:T(8,128)(2,1)} %fusion.58), channel_id=1, replica_groups=mesh['section'=2,'seq'=8,'tp'=8] {'tp'}, use_global_device_ids=true, to_apply=%region_33.34 | all-reduce | flops 24576 | bytes 98304 | tf_op jit(solution)/shard_map/psum | solution.py:219
  525.6 74.1 %all-reduce.15.cloned.1.call-done = bf16[64,1536]{1,0:T(8,128)(2,1)} async-done(((bf16[64,1536]{1,0:T(8,128)(2,1)}), bf16[64,1536]{1,0:T(8,128)(2,1)}) %all-reduce.15.cloned.1.call-update) | async-done | bytes 196624 | tf_op jit(solution)/shard_map/psum | solution.py:199
  608.8 80.7 %all-reduce.17.cloned.1.call-done = bf16[64,1536]{1,0:T(8,128)(2,1)} async-done(((bf16[64,1536]{1,0:T(8,128)(2,1)}), bf16[64,1536]{1,0:T(8,128)(2,1)}) %all-reduce.17.cloned.1.call-update) | async-done | bytes 196624 | tf_op jit(solution)/shard_map/psum | solution.py:213
  692.1 6.2 collective-permute-done.16
  760.3 39.7 %psum.150 = bf16[16,1536]{1,0:T(8,128)(2,1)S(1)} all-reduce(bf16[16,1536]{1,0:T(8,128)(2,1)S(1)} %convolution_convert_fusion.7), channel_id=1, replica_groups=mesh['section'=2,'seq'=8,'tp'=8] {'tp'}, use_global_device_ids=true, to_apply=%region_46.47 | all-reduce | flops 24576 | bytes 98304 | tf_op jit(solution)/shard_map/psum | solution.py:200
  804.5 39.9 %psum.151 = bf16[16,1536]{1,0:T(8,128)(2,1)} all-reduce(bf16[16,1536]{1,0:T(8,128)(2,1)} %fusion.61), channel_id=1, replica_groups=mesh['section'=2,'seq'=8,'tp'=8] {'tp'}, use_global_device_ids=true, to_apply=%region_49.50 | all-reduce | flops 24576 | bytes 98304 | tf_op jit(solution)/shard_map/psum | solution.py:219
  856.7 74.1 %all-reduce.19.cloned.1.call-done = bf16[64,1536]{1,0:T(8,128)(2,1)} async-done(((bf16[64,1536]{1,0:T(8,128)(2,1)}), bf16[64,1536]{1,0:T(8,128)(2,1)}) %all-reduce.19.cloned.1.call-update) | async-done | bytes 196624 | tf_op jit(solution)/shard_map/psum | solution.py:199
  939.9 80.7 %all-reduce.21.cloned.1.call-done = bf16[64,1536]{1,0:T(8,128)(2,1)} async-done(((bf16[64,1536]{1,0:T(8,128)(2,1)}), bf16[64,1536]{1,0:T(8,128)(2,1)}) %all-reduce.21.cloned.1.call-update) | async-done | bytes 196624 | tf_op jit(solution)/shard_map/psum | solution.py:213
  1023.2 6.2 collective-permute-done.25
  1091.4 39.5 %psum.154 = bf16[16,1536]{1,0:T(8,128)(2,1)S(1)} all-reduce(bf16[16,1536]{1,0:T(8,128)(2,1)S(1)} %convolution_convert_fusion.6), channel_id=1, replica_groups=mesh['section'=2,'seq'=8,'tp'=8] {'tp'}, use_global_device_ids=true, to_apply=%region_62.63 | all-reduce | flops 24576 | bytes 98304 | tf_op jit(solution)/shard_map/psum | solution.py:200
  1135.3 39.9 %psum.155 = bf16[16,1536]{1,0:T(8,128)(2,1)} all-reduce(bf16[16,1536]{1,0:T(8,128)(2,1)} %fusion.64), channel_id=1, replica_groups=mesh['section'=2,'seq'=8,'tp'=8] {'tp'}, use_global_device_ids=true, to_apply=%region_65.66 | all-reduce | flops 24576 | bytes 98304 | tf_op jit(solution)/shard_map/psum | solution.py:219
  1189.2 73.2 %all-reduce.23.cloned.1.call-done = bf16[64,1536]{1,0:T(8,128)(2,1)} async-done(((bf16[64,1536]{1,0:T(8,128)(2,1)}), bf16[64,1536]{1,0:T(8,128)(2,1)}) %all-reduce.23.cloned.1.call-update) | async-done | bytes 196624 | tf_op jit(solution)/shard_map/psum | solution.py:199
  1272.4 79.8 %all-reduce.25.cloned.1.call-done = bf16[64,1536]{1,0:T(8,128)(2,1)} async-done(((bf16[64,1536]{1,0:T(8,128)(2,1)}), bf16[64,1536]{1,0:T(8,128)(2,1)}) %all-reduce.25.cloned.1.call-update) | async-done | bytes 196624 | tf_op jit(solution)/shard_map/psum | solution.py:213
  1355.0 6.0 collective-permute-done.34
  1426.5 39.5 %psum.158 = bf16[16,1536]{1,0:T(8,128)(2,1)S(1)} all-reduce(bf16[16,1536]{1,0:T(8,128)(2,1)S(1)} %convolution_convert_fusion.5), channel_id=1, replica_groups=mesh['section'=2,'seq'=8,'tp'=8] {'tp'}, use_global_device_ids=true, to_apply=%region_78.79 | all-reduce | flops 24576 | bytes 98304 | tf_op jit(solution)/shard_map/psum | solution.py:200
  1468.9 78.1 %all-reduce.27.cloned.1.call-done = bf16[64,1536]{1,0:T(8,128)(2,1)} async-done(((bf16[64,1536]{1,0:T(8,128)(2,1)}), bf16[64,1536]{1,0:T(8,128)(2,1)}) %all-reduce.27.cloned.1.call-update) | async-done | bytes 196624 | tf_op jit(solution)/shard_map/psum | solution.py:199
  1558.1 40.4 %psum.159 = bf16[16,1536]{1,0:T(8,128)(2,1)} all-reduce(bf16[16,1536]{1,0:T(8,128)(2,1)S(1)} %fusion.67), channel_id=1, replica_groups=mesh['section'=2,'seq'=8,'tp'=8] {'tp'}, use_global_device_ids=true, to_apply=%region_81.82 | all-reduce | flops 24576 | bytes 98304 | tf_op jit(solution)/shard_map/psum | solution.py:219
  1598.5 38.4 %all-reduce.29.cloned.1.call-done = bf16[64,1536]{1,0:T(8,128)(2,1)} async-done(((bf16[64,1536]{1,0:T(8,128)(2,1)}), bf16[64,1536]{1,0:T(8,128)(2,1)}) %all-reduce.29.cloned.1.call-update) | async-done | bytes 196624 | tf_op jit(solution)/shard_map/psum | solution.py:213
  (673 shorter events, 462.6 us)
Async XLA Ops:
  7.2 74.0 %all-gather.4.cloned.1.call-start = ((), (), s32[]{:S(2)}) async-start(), calls=%async_computation.10 | async-start | bytes 2359296 | tf_op jit(solution)/shard_map/all_gather | solution.py:114
  23.3 36.5 %collective-permute-start = (bf16[2,40,2,192]{3,2,1,0:T(2,128)(2,1)}, bf16[2,40,2,192]{3,2,1,0:T(2,128)(2,1)}, u32[]{:S(2)}, u32[]{:S(2)}) collective-permute-start(bf16[2,40,2,192]{3,2,1,0:T(2,128)(2,1)} %pad_maximum_fusion), channel_id=1, source_target_pairs={{0,8},{8,16},{16,24},{24,32},{32,40},{40,48},{48,56},{56,0},{1,9},... | collective-permute-start | bytes 184328 | tf_op jit(solution)/shard_map/ppermute | solution.py:155
  23.3 36.9 %collective-permute-start.1 = (bf16[2,40,2,192]{3,2,1,0:T(2,128)(2,1)}, bf16[2,40,2,192]{3,2,1,0:T(2,128)(2,1)}, u32[]{:S(2)}, u32[]{:S(2)}) collective-permute-start(bf16[2,40,2,192]{3,2,1,0:T(2,128)(2,1)} %pad_maximum_fusion), channel_id=1, source_target_pairs={{0,56},{8,0},{16,8},{24,16},{32,24},{40,32},{48,40},{56,48},{1,57}... | collective-permute-start | bytes 184328 | tf_op jit(solution)/shard_map/ppermute | solution.py:160
  27.1 241.8 %all-reduce.11.cloned.1.call-start = ((), (), s32[]{:S(2)}) async-start(), calls=%async_computation | async-start | bytes 393216 | tf_op jit(solution)/shard_map/psum | solution.py:199
  185.3 173.4 %all-reduce.13.cloned.1.call-start = ((), (), s32[]{:S(2)}) async-start(), calls=%async_computation.1 | async-start | bytes 393216 | tf_op jit(solution)/shard_map/psum | solution.py:213
  276.6 323.2 %all-reduce.15.cloned.1.call-start = ((), (), s32[]{:S(2)}) async-start(), calls=%async_computation.2 | async-start | bytes 393216 | tf_op jit(solution)/shard_map/psum | solution.py:199
  359.9 7.6 collective-permute-start.7
  372.8 12.0 collective-permute-start.9
  372.8 13.5 collective-permute-start.10
  518.1 171.4 %all-reduce.17.cloned.1.call-start = ((), (), s32[]{:S(2)}) async-start(), calls=%async_computation.3 | async-start | bytes 393216 | tf_op jit(solution)/shard_map/psum | solution.py:213
  607.4 323.4 %all-reduce.19.cloned.1.call-start = ((), (), s32[]{:S(2)}) async-start(), calls=%async_computation.4 | async-start | bytes 393216 | tf_op jit(solution)/shard_map/psum | solution.py:199
  690.8 7.6 collective-permute-start.16
  703.7 12.0 collective-permute-start.18
  703.7 13.5 collective-permute-start.19
  849.2 171.4 %all-reduce.21.cloned.1.call-start = ((), (), s32[]{:S(2)}) async-start(), calls=%async_computation.5 | async-start | bytes 393216 | tf_op jit(solution)/shard_map/psum | solution.py:213
  938.5 323.9 %all-reduce.23.cloned.1.call-start = ((), (), s32[]{:S(2)}) async-start(), calls=%async_computation.6 | async-start | bytes 393216 | tf_op jit(solution)/shard_map/psum | solution.py:199
  1034.7 12.0 collective-permute-start.27
  1034.7 13.5 collective-permute-start.28
  1180.1 172.0 %all-reduce.25.cloned.1.call-start = ((), (), s32[]{:S(2)}) async-start(), calls=%async_computation.7 | async-start | bytes 393216 | tf_op jit(solution)/shard_map/psum | solution.py:213
  1270.1 277.0 %all-reduce.27.cloned.1.call-start = ((), (), s32[]{:S(2)}) async-start(), calls=%async_computation.8 | async-start | bytes 393216 | tf_op jit(solution)/shard_map/psum | solution.py:199
  1353.4 7.6 collective-permute-start.34
  1366.3 15.4 collective-permute-start.36
  1366.3 17.0 %collective-permute-start.37 = (bf16[2,40,2,192]{3,2,1,0:T(2,128)(2,1)}, bf16[2,40,2,192]{3,2,1,0:T(2,128)(2,1)}, u32[]{:S(2)}, u32[]{:S(2)}) collective-permute-start(bf16[2,40,2,192]{3,2,1,0:T(2,128)(2,1)} %pad_maximum_fusion.4), channel_id=1, source_target_pairs={{0,56},{8,0},{16,8},{24,16},{32,24},{40,32},{48,40},{56,48},{1,57}... | collective-permute-start | bytes 184328 | tf_op jit(solution)/shard_map/ppermute | solution.py:160
  1468.3 168.6 %all-reduce.29.cloned.1.call-start = ((), (), s32[]{:S(2)}) async-start(), calls=%async_computation.9 | async-start | bytes 393216 | tf_op jit(solution)/shard_map/psum | solution.py:213
  (123 other events, 4651.4 us)
Sparse Core Ops, SparseCore 0:
  27.2 27.0 all-gather.3
  185.4 83.4 all-reduce.10
  276.7 81.8 all-reduce.12
  518.2 81.5 all-reduce.14
  607.5 81.8 all-reduce.16
  849.3 81.4 all-reduce.18
  938.6 81.8 all-reduce.20
  1180.2 82.1 all-reduce.22
  1270.2 81.8 all-reduce.24
  1468.5 78.5 all-reduce.26
  1554.8 82.0 all-reduce.28
